TPU v7x, 256 devices: a whole 4x4x8 slice. The times are simulated.
256 devices in a mesh: blk: 32 (over x_lo, z, core), own: 8 (over y, x_hi).
Axes of the slice: x: 4 (x_hi: 2, x_lo: 2; x = x_hi * 2 + x_lo), y: 4, z: 8, core: 2. Of those that a mesh axis runs over, the one named last changes fastest.
Arguments:
- embeddings: bfloat16 [32768, 768], P(('blk', 'own')), may hold values from -320 to 320
- centroids: bfloat16 [16384, 768], P('blk'), may hold values from -4 to 4
- log_weight: float32 [16384], P('blk'), may hold values from -0.5 to 1.6
Outputs:
- new_centroids: float32 [16384, 768], P(('blk', 'own'))
- counts: float32 [16384], P(('blk', 'own'))
- log_norm: float32 [32768], P(('blk', 'own'))
All inputs are finite; a program needn't handle non-finite values.
Results may differ from a plain program's by a relative error of at most 0.0015.
Values may be sent and summed in bfloat16 or wider, within the bound.
No kernel may reach another device: no remote copies, remote signals or barrier semaphores. Data moves between devices by JAX's collectives and lax.ppermute only.
A program may use at most 64 MiB of HBM per device.

v0:
```python
import math
import jax
import jax.numpy as jnp
from jax import lax
from jax.sharding import PartitionSpec as P

prior_mass = 1.0


def copy_for_each(array, axis):
    copies = jnp.broadcast_to(array, (lax.axis_size(axis), *array.shape))
    return lax.all_to_all(copies, axis, split_axis=0, concat_axis=0, tiled=True)


def collected_together(array, axis):
    leaves = jax.tree.leaves(array)
    turns = sorted(range(len(leaves)), key=lambda k: -leaves[k].size)
    width = (1, *leaves[turns[0]].shape)[-1]
    lines = [
        jnp.pad(leaves[k].reshape(-1), (0, -leaves[k].size % width)).reshape(-1, width)
        for k in turns
    ]
    both, at, found = (copy_for_each(jnp.concatenate(lines), axis), 0, {})
    for k, line in zip(turns, lines):
        share = both[:, at : at + len(line)].reshape(len(both), -1)
        found[k] = share[:, : leaves[k].size].reshape(-1, *leaves[k].shape)
        at += len(line)
    numbers = iter(range(len(leaves)))
    return jax.tree.map(lambda _: found[next(numbers)], array)


def combined_pairwise(pieces, combine):
    while len(jax.tree.leaves(pieces)[0]) > 1:
        pieces = jax.vmap(combine)(
            *(jax.tree.map(lambda part: part[side::2], pieces) for side in (0, 1))
        )
    return jax.tree.map(lambda part: part[0], pieces)


def merged(array, axis, combine):
    pieces = collected_together(array, axis)
    return combined_pairwise(pieces, combine)


def cut_along(array, dim, count):
    lengths = array.shape
    tiles = array.reshape(*lengths[:dim], count, lengths[dim] // count, *lengths[dim + 1 :])
    return jnp.moveaxis(tiles, dim, 0)


def sent_and_summed(array, axis, dim):
    count = lax.axis_size(axis)
    tiles = lax.all_to_all(cut_along(array, dim, count), axis, 0, 0, tiled=True)
    return jnp.sum(tiles, axis=0)


def score_rows(row_block, centroids, half_sq, log_weight, scale_root):
    dots = lax.dot_general(
        row_block, centroids, (((1,), (1,)), ((), ())), preferred_element_type=jnp.float32
    )
    return (dots - half_sq[None, :]) / scale_root + log_weight[None, :]


def local(embeddings, centroids, log_weight):
    row_count, feat_dim = embeddings.shape
    local_count = centroids.shape[0]
    centre_vals = centroids.astype(jnp.float32)
    half_sq = 0.5 * jnp.sum(centre_vals * centre_vals, axis=1)
    scale_root = math.sqrt(feat_dim)
    logits = score_rows(
        lax.all_gather(embeddings, "blk", axis=0, tiled=True),
        centroids,
        half_sq,
        log_weight,
        scale_root,
    )
    peak_val = jnp.max(logits, axis=1)
    peak_part = peak_val
    mass_part = jnp.sum(jnp.exp(logits - peak_val[:, None]), axis=1)
    peak_val = peak_part
    mass_sum = mass_part

    def combine(first_pair, later_pair):
        joined = jnp.maximum(first_pair[0], later_pair[0])
        return (
            joined,
            first_pair[1] * jnp.exp(first_pair[0] - joined)
            + later_pair[1] * jnp.exp(later_pair[0] - joined),
        )

    peak_val, mass_sum = merged((peak_val, mass_sum), "blk", combine)
    log_total = peak_val + jnp.log(mass_sum)
    empty_sums = jnp.zeros((local_count, feat_dim), jnp.float32)
    empty_counts = jnp.zeros((local_count,), jnp.float32)
    row_block = lax.all_gather(embeddings, "blk", axis=0, tiled=True)
    logits = score_rows(row_block, centroids, half_sq, log_weight, scale_root)
    resp_vals = jnp.exp(logits - log_total[:, None])
    contrib = lax.dot_general(
        resp_vals.astype(jnp.bfloat16),
        row_block,
        (((0,), (0,)), ((), ())),
        preferred_element_type=jnp.float32,
    )
    contrib, count_part = (contrib, jnp.sum(resp_vals, axis=0))
    weighted = contrib
    counts = (empty_sums, empty_counts)[1] + count_part
    weighted, counts = (sent_and_summed(weighted, "own", 0), sent_and_summed(counts, "own", 0))
    owned_count = local_count // lax.axis_size("own")
    own_index = lax.axis_index("own")
    own_centres = lax.dynamic_slice_in_dim(centre_vals, own_index * owned_count, owned_count, 0)
    updated = (weighted + prior_mass * own_centres) / (counts[:, None] + prior_mass)
    log_norm = lax.dynamic_slice_in_dim(log_total, lax.axis_index("blk") * row_count, row_count, 0)
    return (updated, counts, log_norm)


def solution(mesh):
    placed = (P(("blk", "own"), None), P("blk", None), P("blk"))
    return jax.shard_map(
        local,
        mesh=mesh,
        in_specs=placed,
        out_specs=(P(("blk", "own"), None), P(("blk", "own")), P(("blk", "own"))),
        check_vma=False,
    )
```

profile of v0, /device:TPU:32, one launch (start us, length us, event | category | flops | bytes accessed | tf_op | source)
XLA Modules:
  0.0 191.8 jit_solution(2781830788650535467)
XLA Ops:
  7.2 0.7 all-gather.2.cloned.1.call-update
  7.9 1.4 multiply_reduce_fusion
  9.3 72.4 %all-gather.2.cloned.1.call-done = bf16[4096,768]{1,0:T(8,128)(2,1)} async-done(((bf16[128,768]{1,0:T(8,128)(2,1)}), bf16[4096,768]{1,0:T(8,128)(2,1)}) %all-gather.2.cloned.1.call-update) | async-done | bytes 6291472 | tf_op jit(solution)/shard_map/all_gather | solution.py:95
  81.6 5.9 %fusion.8 = (f32[4096]{0:T(1024)S(1)}, f32[4096,512]{0,1:T(8,128)S(1)}) fusion(f32[512]{0:T(512)} %param.5, f32[512]{0:T(512)S(1)} %broadcast_multiply_fusion, bf16[4096,768]{1,0:T(8,128)(2,1)} %all-gather.2.cloned.1.call-done, bf16[512,768]{1,0:T(8,128)(2,1)} %param.4), kind=kOutput, calls=%fused_computation.26 | convolution fusion | flops 3229609984 | bytes 15486976 | tf_op jit(solution)/shard_map/dot_general | solution.py:58
  87.5 3.2 %copy-done = f32[4096,512]{0,1:T(8,128)} copy-done((f32[4096,512]{0,1:T(8,128)}, f32[4096,512]{0,1:T(8,128)S(1)}, u32[]{:S(2)}) %copy-start) | copy-done | bytes 8388632
  90.8 1.3 exponential_reduce_fusion
  92.1 0.5 broadcast_in_dim.2
  92.6 36.4 %all_to_all.19 = f32[32,2,4096]{2,1,0:T(2,128)S(1)} all-to-all(f32[32,2,4096]{2,1,0:T(2,128)S(1)} %broadcast_in_dim.2), channel_id=1, replica_groups=mesh['blk'=32,'own'=8] {'blk'}, dimensions={0} | all-to-all | bytes 2097152 | tf_op jit(solution)/shard_map/all_to_all | solution.py:12
  129.0 0.8 fusion.7
  129.8 0.6 copy_bitcast_fusion
  130.4 0.1 slice.71
  130.6 0.1 slice.72
  130.8 0.1 slice.82
  130.9 0.1 slice.83
  132.2 0.1 slice.77
  132.8 4.6 %fusion = f32[512]{0:T(512)S(1)} fusion(f32[4096,512]{0,1:T(8,128)} %copy-done, f32[4096]{0:T(1024)S(1)} %bitcast.15), kind=kLoop, calls=%fused_computation.3 | loop fusion | flops 4193792 | bytes 8407040 | tf_op jit(solution)/shard_map/reduce_sum | solution.py:104
  137.4 0.7 all_to_all.14
  138.1 6.4 %all-to-all-start.2 = ((f32[8,1,64]{2,1,0:T(1,128)}), f32[8,1,64]{2,1,0:T(1,128)S(1)}, u32[]{:S(2)}, u32[]{:S(2)}) async-start(f32[8,1,64]{2,1,0:T(1,128)} %all_to_all.14), calls=%async_computation.2 | async-start | bytes 8192 | tf_op jit(solution)/shard_map/all_to_all | solution.py:53
  144.5 9.9 %fusion.2 = f32[512,768]{1,0:T(8,128)} fusion(bf16[4096,768]{1,0:T(8,128)(2,1)} %all-gather.2.cloned.1.call-done, f32[4096,512]{0,1:T(8,128)} %copy-done, f32[4096]{0:T(1024)S(1)} %bitcast.16), kind=kOutput, calls=%fused_computation.5 | convolution fusion | flops 3225419776 | bytes 16269312 | tf_op jit(solution)/shard_map/dot_general | solution.py:98
  154.4 7.2 %all-to-all-start.1 = ((f32[8,64,768]{2,1,0:T(8,128)}), f32[8,64,768]{2,1,0:T(8,128)S(1)}, u32[]{:S(2)}, u32[]{:S(2)}) async-start(f32[8,64,768]{2,1,0:T(8,128)} %bitcast.14), calls=%async_computation.1 | async-start | bytes 3145728 | tf_op jit(solution)/shard_map/all_to_all | solution.py:53
  161.6 1.3 convert_element_type.6
  162.8 0.5 dynamic-slice_bitcast_fusion
  163.4 19.7 %all-to-all-done.1 = f32[8,64,768]{2,1,0:T(8,128)S(1)} async-done(((f32[8,64,768]{2,1,0:T(8,128)}), f32[8,64,768]{2,1,0:T(8,128)S(1)}, u32[]{:S(2)}, u32[]{:S(2)}) %all-to-all-start.1) | async-done | bytes 1572896 | tf_op jit(solution)/shard_map/all_to_all | solution.py:53
  183.2 1.7 add_divide_fusion
  (28 shorter events, 1.7 us)
Async XLA Ops:
  7.2 74.5 %all-gather.2.cloned.1.call-start = ((), (), s32[]{:S(2)}) async-start(), calls=%async_computation.3 | async-start | bytes 6488064 | tf_op jit(solution)/shard_map/all_gather | solution.py:95
  87.5 3.2 %copy-start = (f32[4096,512]{0,1:T(8,128)}, f32[4096,512]{0,1:T(8,128)S(1)}, u32[]{:S(2)}) copy-start(f32[4096,512]{0,1:T(8,128)S(1)} %get-tuple-element.14) | copy-start | bytes 25165828
  138.1 16.3 %all-to-all-start.2 = ((f32[8,1,64]{2,1,0:T(1,128)}), f32[8,1,64]{2,1,0:T(1,128)S(1)}, u32[]{:S(2)}, u32[]{:S(2)}) async-start(f32[8,1,64]{2,1,0:T(1,128)} %all_to_all.14), calls=%async_computation.2 | async-start | bytes 8192 | tf_op jit(solution)/shard_map/all_to_all | solution.py:53
  144.5 17.1 %copy-start.1 = (bf16[512,768]{1,0:T(8,128)(2,1)S(1)}, bf16[512,768]{1,0:T(8,128)(2,1)}, u32[]{:S(2)}) copy-start(bf16[512,768]{1,0:T(8,128)(2,1)} %param.4) | copy-start | bytes 2359300
  154.4 28.7 %all-to-all-start.1 = ((f32[8,64,768]{2,1,0:T(8,128)}), f32[8,64,768]{2,1,0:T(8,128)S(1)}, u32[]{:S(2)}, u32[]{:S(2)}) async-start(f32[8,64,768]{2,1,0:T(8,128)} %bitcast.14), calls=%async_computation.1 | async-start | bytes 3145728 | tf_op jit(solution)/shard_map/all_to_all | solution.py:53
  163.4 21.5 %copy-start.2 = (f32[64]{0:T(128)}, f32[64]{0:T(128)S(1)}, u32[]{:S(2)}) copy-start(f32[64]{0:T(128)S(1)} %reduce_sum.49) | copy-start | bytes 772
Sparse Core Ops, SparseCore 0:
  9.9 71.7 all-gather.1
where the time goes:
time: 192 us
  waiting for transfers between devices  92.8 us (48%)
  blocking collectives  36.4 us (19%)
  matrix products  15.8 us (8%)
  between operations  14.3 us (7%)
  starting transfers between devices  13.7 us (7%)
  other arithmetic  10.7 us (6%)
  local copies, waits for them, and re-layouts  8.15 us (4%)
    all_gather x1, waiting for transfers between devices, local(): row_block = lax.all_gather(embeddings, 'blk', axis=0, tiled=True)  72.4 us
    all_to_all x1, blocking collectives, copy_for_each(): return lax.all_to_all(copies, axis, split_axis=0, concat_axis=0, tiled=True)  36.4 us
    all_to_all x2, waiting for transfers between devices, sent_and_summed(): tiles = lax.all_to_all(cut_along(array, dim, count), axis, 0, 0, tiled=True)  19.7 us
    all_to_all x2, starting transfers between devices, sent_and_summed(): tiles = lax.all_to_all(cut_along(array, dim, count), axis, 0, 0, tiled=True)  13.6 us
    dot_general x1, matrix products, local(): lax.dot_general(resp_vals.astype(jnp.bfloat16), row_block, (((0,), (0,)),...  9.89 us
    dot_general x1, matrix products, score_rows(): lax.dot_general(row_block, centroids, (((1,), (1,)), ((), ())), preferred...  5.87 us
    reduce_sum x1, other arithmetic, local(): contrib, count_part = (contrib, jnp.sum(resp_vals, axis=0))  4.57 us
  transfers between devices with their start and end apart: 3, of which 2 were waited for; matrix products, arithmetic and copies ran while one was open for 7% of the time, Pallas kernels for 0%

commit v1 on v0

--- a/solution.py
+++ b/solution.py
@@ -92,7 +92,9 @@
     log_total = peak_val + jnp.log(mass_sum)
     empty_sums = jnp.zeros((local_count, feat_dim), jnp.float32)
     empty_counts = jnp.zeros((local_count,), jnp.float32)
-    row_block = lax.all_gather(embeddings, "blk", axis=0, tiled=True)
+    row_block = jnp.concatenate(
+        lax.all_to_all(jnp.stack([embeddings] * lax.axis_size("blk")), "blk", 0, 0), axis=0
+    )
     logits = score_rows(row_block, centroids, half_sq, log_weight, scale_root)
     resp_vals = jnp.exp(logits - log_total[:, None])
     contrib = lax.dot_general(

time: 192 us -> 338 us (1.76); the launches traced: 192 us -> 334 us
  waiting for transfers between devices: 92.8 us -> 226 us
  matrix products: 15.8 us -> 22.6 us
  starting transfers between devices: 13.7 us -> 18.3 us
  other arithmetic: 10.7 us -> 7.24 us
    all_to_all x0 -> x1, waiting for transfers between devices: none -> 134 us  [local(): lax.all_to_all(jnp.stack([embeddings] * lax.axis_size('blk')), 'blk', 0, 0)]
    dot_general x1 -> x2, matrix products: 5.87 us -> 14 us  [score_rows(): lax.dot_general(row_block, centroids, (((1,), (1,)), ((), ())), preferred...]
    all_to_all x0 -> x1, starting transfers between devices: none -> 4.69 us  [local(): lax.all_to_all(jnp.stack([embeddings] * lax.axis_size('blk')), 'blk', 0, 0)]
    reduce_sum x1 -> x0, other arithmetic: 4.57 us -> none  [local(): contrib, count_part = (contrib, jnp.sum(resp_vals, axis=0))]
  transfers between devices with their start and end apart: 3 -> 4, of which waited for: 2 -> 3; matrix products, arithmetic and copies ran while one was open for 7% -> 5% of each run, Pallas kernels for 0% -> 0%
where the time goes in v1:
time: 338 us; the launch traced here: 334 us
  waiting for transfers between devices  226 us (67%)
  blocking collectives  36.4 us (11%)
  matrix products  22.6 us (7%)
  starting transfers between devices  18.3 us (5%)
  between operations  14.3 us (4%)
  local copies, waits for them, and re-layouts  8.67 us (3%)
  other arithmetic  7.24 us (2%)
    all_to_all x1, waiting for transfers between devices, local(): lax.all_to_all(jnp.stack([embeddings] * lax.axis_size('blk')), 'blk', 0, 0)  134 us
    all_gather x1, waiting for transfers between devices, local(): lax.all_gather(embeddings, 'blk', axis=0, tiled=True)  72.4 us
    all_to_all x1, blocking collectives, copy_for_each(): return lax.all_to_all(copies, axis, split_axis=0, concat_axis=0, tiled=True)  36.4 us
    all_to_all x2, waiting for transfers between devices, sent_and_summed(): tiles = lax.all_to_all(cut_along(array, dim, count), axis, 0, 0, tiled=True)  19.1 us
    dot_general x2, matrix products, score_rows(): lax.dot_general(row_block, centroids, (((1,), (1,)), ((), ())), preferred...  14 us
    all_to_all x2, starting transfers between devices, sent_and_summed(): tiles = lax.all_to_all(cut_along(array, dim, count), axis, 0, 0, tiled=True)  13.6 us
    dot_general x1, matrix products, local(): lax.dot_general(resp_vals.astype(jnp.bfloat16), row_block, (((0,), (0,)),...  8.61 us
  transfers between devices with their start and end apart: 4, of which 3 were waited for; matrix products, arithmetic and copies ran while one was open for 5% of the time, Pallas kernels for 0%

profile of v1, /device:TPU:32, one launch (start us, length us, event | category | flops | bytes accessed | tf_op | source)
XLA Modules:
  0.0 333.6 jit_solution(16135556141622881189)
XLA Ops:
  7.2 0.7 all-gather.2.cloned.1.call-update
  7.9 1.4 multiply_reduce_fusion
  9.3 72.4 %all-gather.2.cloned.1.call-done = bf16[4096,768]{1,0:T(8,128)(2,1)} async-done(((bf16[128,768]{1,0:T(8,128)(2,1)}), bf16[4096,768]{1,0:T(8,128)(2,1)}) %all-gather.2.cloned.1.call-update) | async-done | bytes 6291472 | tf_op jit(solution)/shard_map/all_gather | solution.py:71
  81.6 5.8 %fusion = (f32[4096]{0:T(1024)S(1)}, f32[4096,512]{0,1:T(8,128)S(1)}) fusion(f32[512]{0:T(512)} %param.5, f32[512]{0:T(512)S(1)} %broadcast_multiply_fusion, bf16[4096,768]{1,0:T(8,128)(2,1)} %all-gather.2.cloned.1.call-done, bf16[512,768]{1,0:T(8,128)(2,1)} %param.4), kind=kOutput, calls=%fused_computation.3 | convolution fusion | flops 3229609984 | bytes 15486976 | tf_op jit(solution)/shard_map/dot_general | solution.py:58
  87.5 2.4 exponential_reduce_fusion
  90.0 0.5 broadcast_in_dim.2
  90.4 36.4 %all_to_all.24 = f32[32,2,4096]{2,1,0:T(2,128)S(1)} all-to-all(f32[32,2,4096]{2,1,0:T(2,128)S(1)} %broadcast_in_dim.2), channel_id=1, replica_groups=mesh['blk'=32,'own'=8] {'blk'}, dimensions={0} | all-to-all | bytes 2097152 | tf_op jit(solution)/shard_map/all_to_all | solution.py:12
  126.9 3.4 %stack.2 = bf16[32,128,768]{2,1,0:T(8,128)(2,1)} broadcast(bf16[128,768]{1,0:T(8,128)(2,1)S(1)} %copy-done.1), dimensions={1,2} | broadcast | bytes 6488064 | tf_op jit(solution)/shard_map/stack | solution.py:96
  130.2 4.7 %all-to-all-start = ((bf16[32,128,768]{2,1,0:T(8,128)(2,1)}), bf16[32,128,768]{2,1,0:T(8,128)(2,1)}, u32[]{:S(2)}, u32[]{:S(2)}) async-start(bf16[32,128,768]{2,1,0:T(8,128)(2,1)} %stack.2), calls=%async_computation | async-start | bytes 12582912 | tf_op jit(solution)/shard_map/all_to_all | solution.py:96
  134.9 1.2 fusion.4
  136.1 0.6 copy_bitcast_fusion
  136.7 0.1 slice.71
  136.9 0.1 slice.72
  137.0 0.1 slice.82
  139.1 133.8 %all-to-all-done = bf16[32,128,768]{2,1,0:T(8,128)(2,1)} async-done(((bf16[32,128,768]{2,1,0:T(8,128)(2,1)}), bf16[32,128,768]{2,1,0:T(8,128)(2,1)}, u32[]{:S(2)}, u32[]{:S(2)}) %all-to-all-start) | async-done | bytes 6291488 | tf_op jit(solution)/shard_map/all_to_all | solution.py:96
  272.9 8.1 %fusion.3 = (f32[512]{0:T(512)S(1)}, bf16[4096,512]{0,1:T(8,128)(2,1)}) fusion(f32[4096]{0:T(1024)S(1)} %bitcast.24, f32[512]{0:T(512)S(1)} %copy-done.2, f32[512]{0:T(512)S(1)} %broadcast_multiply_fusion, bf16[4096,768]{1,0:T(8,128)(2,1)} %bitcast, bf16[512,768]{1,0:T(8,128)(2,1)S(1)} %copy-done), kind=kOutput, calls=%fused_computation.22 | convolution fusion | flops 3233807872 | bytes 11294720 | tf_op jit(solution)/shard_map/dot_general | solution.py:58
  281.0 0.7 all_to_all.18
  281.7 6.4 %all-to-all-start.3 = ((f32[8,1,64]{2,1,0:T(1,128)}), f32[8,1,64]{2,1,0:T(1,128)S(1)}, u32[]{:S(2)}, u32[]{:S(2)}) async-start(f32[8,1,64]{2,1,0:T(1,128)} %all_to_all.18), calls=%async_computation.3 | async-start | bytes 8192 | tf_op jit(solution)/shard_map/all_to_all | solution.py:53
  288.1 8.6 %fusion.5 = f32[8,64,768]{2,1,0:T(8,128)} fusion(bf16[8,64,4096]{2,1,0:T(8,128)(2,1)} %bitcast.26, bf16[4096,768,1]{1,0,2:T(8,128)(2,1)} %bitcast.7), kind=kOutput, calls=%fused_computation.24 | convolution fusion | flops 3221225472 | bytes 12058624 | tf_op jit(solution)/shard_map/dot_general | solution.py:100
  296.7 7.2 %all-to-all-start.2 = ((f32[8,64,768]{2,1,0:T(8,128)}), f32[8,64,768]{2,1,0:T(8,128)S(1)}, u32[]{:S(2)}, u32[]{:S(2)}) async-start(f32[8,64,768]{2,1,0:T(8,128)} %fusion.5), calls=%async_computation.2 | async-start | bytes 3145728 | tf_op jit(solution)/shard_map/all_to_all | solution.py:53
  304.0 1.3 convert_element_type.7
  305.2 0.5 dynamic-slice_bitcast_fusion
  305.8 19.1 %all-to-all-done.2 = f32[8,64,768]{2,1,0:T(8,128)S(1)} async-done(((f32[8,64,768]{2,1,0:T(8,128)}), f32[8,64,768]{2,1,0:T(8,128)S(1)}, u32[]{:S(2)}, u32[]{:S(2)}) %all-to-all-start.2) | async-done | bytes 1572896 | tf_op jit(solution)/shard_map/all_to_all | solution.py:53
  325.0 1.7 add_divide_fusion
  (33 shorter events, 2.0 us)
Async XLA Ops:
  7.2 74.5 %all-gather.2.cloned.1.call-start = ((), (), s32[]{:S(2)}) async-start(), calls=%async_computation.4 | async-start | bytes 6488064 | tf_op jit(solution)/shard_map/all_gather | solution.py:71
  9.3 78.2 %copy-start.2 = (f32[512]{0:T(512)S(1)}, f32[512]{0:T(512)}, u32[]{:S(2)}) copy-start(f32[512]{0:T(512)} %param.5) | copy-start | bytes 6148
  87.5 39.4 %copy-start.1 = (bf16[128,768]{1,0:T(8,128)(2,1)S(1)}, bf16[128,768]{1,0:T(8,128)(2,1)}, u32[]{:S(2)}) copy-start(bf16[128,768]{1,0:T(8,128)(2,1)} %param.3) | copy-start | bytes 589828
  130.2 142.7 %all-to-all-start = ((bf16[32,128,768]{2,1,0:T(8,128)(2,1)}), bf16[32,128,768]{2,1,0:T(8,128)(2,1)}, u32[]{:S(2)}, u32[]{:S(2)}) async-start(bf16[32,128,768]{2,1,0:T(8,128)(2,1)} %stack.2), calls=%async_computation | async-start | bytes 12582912 | tf_op jit(solution)/shard_map/all_to_all | solution.py:96
  134.9 138.0 %copy-start = (bf16[512,768]{1,0:T(8,128)(2,1)S(1)}, bf16[512,768]{1,0:T(8,128)(2,1)}, u32[]{:S(2)}) copy-start(bf16[512,768]{1,0:T(8,128)(2,1)} %param.4) | copy-start | bytes 2359300
  281.7 15.0 %all-to-all-start.3 = ((f32[8,1,64]{2,1,0:T(1,128)}), f32[8,1,64]{2,1,0:T(1,128)S(1)}, u32[]{:S(2)}, u32[]{:S(2)}) async-start(f32[8,1,64]{2,1,0:T(1,128)} %all_to_all.18), calls=%async_computation.3 | async-start | bytes 8192 | tf_op jit(solution)/shard_map/all_to_all | solution.py:53
  296.7 28.2 %all-to-all-start.2 = ((f32[8,64,768]{2,1,0:T(8,128)}), f32[8,64,768]{2,1,0:T(8,128)S(1)}, u32[]{:S(2)}, u32[]{:S(2)}) async-start(f32[8,64,768]{2,1,0:T(8,128)} %fusion.5), calls=%async_computation.2 | async-start | bytes 3145728 | tf_op jit(solution)/shard_map/all_to_all | solution.py:53
  305.8 21.0 %copy-start.3 = (f32[64]{0:T(128)}, f32[64]{0:T(128)S(1)}, u32[]{:S(2)}) copy-start(f32[64]{0:T(128)S(1)} %reduce_sum.49) | copy-start | bytes 772
Sparse Core Ops, SparseCore 0:
  9.9 71.7 all-gather.1
